TPU v7x, 128 devices: a whole 4x4x4 slice. The times are simulated.
128 devices in a mesh: tile: 32 (over x, z, core), cuts: 4 (over y).
Axes of the slice: x: 4, y: 4, z: 4, core: 2. Of those that a mesh axis runs over, the one named last changes fastest.
Arguments:
- amplitudes: float32 [1024, 128, 128], P(('tile', 'cuts')), may hold values from 0 to 2
- positions: int32 [1024, 2], replicated, may hold values from 0 to 3968, as said below
- probe_field: float32 [2, 128, 128], replicated, may hold values from -4 to 4
- object_slices: float32 [4, 2, 256, 4096], P('cuts', None, None, 'tile'), may hold values from -1 to 1, as said below
Outputs:
- refined_object: float32 [4, 2, 256, 4096], P('cuts', None, None, 'tile')
Inputs may be any that keep to these rules, and one draw needn't show every extreme that they name: `positions`: rows lie in 0 .. 128; every frame's 128 columns lie inside the 4096 columns. A frame's owner tile is its column // 128. Frames are read in blocks of 8 consecutive frames, one block per device of tile+cuts in mesh order; one block holds at most 2 frames of any owner tile, and some block holds exactly 2. For every cuts index, the blocks of that index hold at most 16 frames of any one owner tile, and in every draw some owner tile receives exactly 16 from them. `object_slices`: transmissions have modulus at most 1.
All inputs are finite; a program needn't handle non-finite values.
Results may differ from a plain program's by a relative error of at most 0.015.
Values may be sent and summed in bfloat16 or wider, within the bound.
A program may use at most 128 MiB of HBM per device.

v0:
```python
import math
import jax
import jax.numpy as jnp
from jax import lax
from jax.sharding import PartitionSpec as P

ITERS = 2
STEP_SIZE = 0.05
AMPLITUDE_FLOOR = 0.25


def passed_along(x, axis, by):
    peers = lax.axis_size(axis)
    pairs = [(i, i + by) for i in range(peers) if 0 <= i + by < peers]
    return lax.ppermute(x, axis, pairs)


def block_table(real_part, imag_part):
    upper = jnp.stack([real_part, imag_part], axis=1)
    lower = jnp.stack([-imag_part, real_part], axis=1)
    return jnp.stack([upper, lower], axis=0).astype(jnp.bfloat16)


def make_tables(frame_side):
    highest = lax.Precision.HIGHEST
    index = jnp.arange(frame_side, dtype=jnp.int32)
    product = index[:, None] * index[None, :] % frame_side
    angle = product.astype(jnp.float32) * (2.0 * math.pi / frame_side)
    norm_scale = 1.0 / math.sqrt(frame_side)
    four_real = jnp.cos(angle) * norm_scale
    four_imag = -jnp.sin(angle) * norm_scale
    centred = (index + frame_side // 2) % frame_side - frame_side // 2
    chirp = -math.pi * (centred * centred).astype(jnp.float32) / (4.0 * frame_side)
    chirp_real = jnp.cos(chirp)
    chirp_imag = jnp.sin(chirp)
    left_real = four_real * chirp_real[None, :] + four_imag * chirp_imag[None, :]
    left_imag = four_real * chirp_imag[None, :] - four_imag * chirp_real[None, :]
    prop_real = jnp.dot(left_real, four_real, precision=highest) - jnp.dot(
        left_imag, four_imag, precision=highest
    )
    prop_imag = jnp.dot(left_real, four_imag, precision=highest) + jnp.dot(
        left_imag, four_real, precision=highest
    )
    return (
        block_table(four_real, four_imag),
        block_table(four_real, -four_imag),
        block_table(prop_real, prop_imag),
        block_table(prop_real, -prop_imag),
    )


def right_product(field, table):
    return jnp.einsum(
        "fcij,cjdk->fdik", field.astype(jnp.bfloat16), table, preferred_element_type=jnp.float32
    )


def two_sided(field, table):
    first = right_product(field, table)
    second = right_product(jnp.swapaxes(first, -1, -2), table)
    return jnp.swapaxes(second, -1, -2)


def complex_times(left, right):
    real_part = left[..., 0, :, :] * right[..., 0, :, :] - left[..., 1, :, :] * right[..., 1, :, :]
    imag_part = left[..., 0, :, :] * right[..., 1, :, :] + left[..., 1, :, :] * right[..., 0, :, :]
    return jnp.stack([real_part, imag_part], axis=-3)


def conj_times(left, right):
    real_part = left[..., 0, :, :] * right[..., 0, :, :] + left[..., 1, :, :] * right[..., 1, :, :]
    imag_part = left[..., 0, :, :] * right[..., 1, :, :] - left[..., 1, :, :] * right[..., 0, :, :]
    return jnp.stack([real_part, imag_part], axis=-3)


def frame_patches(windows, probe_field, measured, tables):
    four, four_conj, prop, prop_conj = tables
    slice_count = windows.shape[1]
    wave = complex_times(probe_field[None], windows[:, 0].astype(jnp.float32))
    fields = []
    for level in range(1, slice_count):
        moved = two_sided(wave, prop)
        fields.append(moved)
        wave = complex_times(windows[:, level].astype(jnp.float32), moved)
    far = two_sided(wave, four)
    magnitude = jnp.sqrt(far[:, 0] * far[:, 0] + far[:, 1] * far[:, 1])
    factor = 1.0 - measured / jnp.maximum(magnitude, AMPLITUDE_FLOOR)
    back = two_sided(far * factor[:, None], four_conj)
    patches = [None] * slice_count
    for level in range(slice_count - 1, 0, -1):
        patches[level] = conj_times(fields[level - 1], back)
        back = two_sided(conj_times(windows[:, level].astype(jnp.float32), back), prop_conj)
    patches[0] = conj_times(probe_field[None], back)
    return jnp.stack(patches, axis=1)


def cut_windows(panel, frame_rows, frame_cols, frame_side):
    zero_index = jnp.zeros((), jnp.int32)

    def window_at(row_start, col_start):
        start = (zero_index, zero_index, row_start, col_start)
        return lax.dynamic_slice(
            panel, start, (panel.shape[0], panel.shape[1], frame_side, frame_side)
        )

    return jax.vmap(window_at)(frame_rows, frame_cols)


def place_patches(panel_shape, patches, frame_rows, frame_cols, weights):
    panel_height = panel_shape[-2]
    panel_width = panel_shape[-1]
    frame_side = patches.shape[-1]
    offsets = jnp.arange(frame_side, dtype=jnp.int32)
    col_target = frame_cols[:, None] + offsets[None, :]
    col_onehot = (
        col_target[:, :, None] == jnp.arange(panel_width, dtype=jnp.int32)[None, None, :]
    ).astype(jnp.bfloat16)
    row_target = frame_rows[:, None] + offsets[None, :]
    row_onehot = (
        jnp.arange(panel_height, dtype=jnp.int32)[:, None, None] == row_target[None, :, :]
    ).astype(jnp.bfloat16)
    remain = patches * weights[:, None, None, None, None]
    gathered_sum = jnp.zeros(panel_shape, jnp.float32)
    for piece_index in range(3):
        piece_part = remain.astype(jnp.bfloat16)
        remain = remain - piece_part.astype(jnp.float32)
        placed_cols = jnp.einsum(
            "fscij,fjk->fscik", piece_part, col_onehot, preferred_element_type=jnp.float32
        ).astype(jnp.bfloat16)
        gathered_sum = gathered_sum + jnp.einsum(
            "hfi,fscik->schk", row_onehot, placed_cols, preferred_element_type=jnp.float32
        )
    return gathered_sum


def reduce_gradient(term_part):
    return lax.psum_scatter(term_part, "cuts", scatter_dimension=0, tiled=True)


def add_rim(main_part, moved_rim):
    extra = main_part.shape[-1] - moved_rim.shape[-1]
    return main_part + moved_rim


def body(amplitudes, positions, probe_field, object_slices):
    tile_count = lax.axis_size("tile")
    cut_count = lax.axis_size("cuts")
    tile_id = lax.axis_index("tile")
    cut_id = lax.axis_index("cuts")
    frame_side = probe_field.shape[-1]
    frames_held = amplitudes.shape[0]
    tile_width = object_slices.shape[-1]
    total_frames = positions.shape[0]
    reader_count = total_frames // frames_held
    capacity = max(2, 2 * frames_held // tile_count)
    max_load = 2 * frames_held
    row_list = positions[:, 0]
    col_list = positions[:, 1]
    owner = col_list // tile_width
    owner_grid = owner.reshape(reader_count, frames_held)
    earlier = jnp.tril(jnp.ones((frames_held, frames_held), jnp.int32), -1)
    same_owner = (owner_grid[:, :, None] == owner_grid[:, None, :]).astype(jnp.int32)
    slot_grid = jnp.sum(same_owner * earlier[None], axis=2)
    slot_list = slot_grid.reshape(total_frames)
    reader_self = tile_id * cut_count + cut_id
    my_owner = lax.dynamic_index_in_dim(owner_grid, reader_self, 0, keepdims=False)
    my_slot = lax.dynamic_index_in_dim(slot_grid, reader_self, 0, keepdims=False)
    target = my_owner * capacity + my_slot
    source = (
        jnp.full((tile_count * capacity,), frames_held, jnp.int32)
        .at[target]
        .set(jnp.arange(frames_held, dtype=jnp.int32))
    )
    padded = jnp.concatenate(
        [amplitudes, jnp.zeros((1, frame_side, frame_side), amplitudes.dtype)], axis=0
    )
    outgoing = jnp.take(padded, source, axis=0).reshape(
        tile_count, capacity, frame_side, frame_side
    )
    incoming = lax.all_to_all(outgoing, "tile", split_axis=0, concat_axis=0, tiled=True)
    reader_of = jnp.arange(total_frames, dtype=jnp.int32) // frames_held
    mine = (owner == tile_id) & (reader_of % cut_count == cut_id)
    rank_list = jnp.cumsum(mine.astype(jnp.int32)) - 1
    spot_list = jnp.where(mine, rank_list, max_load)
    chosen = (
        jnp.zeros((max_load,), jnp.int32)
        .at[spot_list]
        .set(jnp.arange(total_frames, dtype=jnp.int32), mode="drop")
    )
    live_weight = jnp.zeros((max_load,), jnp.float32).at[spot_list].set(1.0, mode="drop")
    flat_slot = reader_of // cut_count * capacity + slot_list
    picked = jnp.take(flat_slot, chosen)
    frames_in = jnp.take(
        incoming.reshape(tile_count * capacity, frame_side, frame_side), picked, axis=0
    )
    frame_rows = jnp.take(row_list, chosen)
    frame_cols = jnp.take(col_list, chosen) - tile_id * tile_width
    tables = make_tables(frame_side)
    current = object_slices
    for turn in range(ITERS):
        stacked = lax.all_gather(current.astype(jnp.bfloat16), "cuts", axis=0, tiled=True)
        next_rim = passed_along(stacked, "tile", -1)
        panel = jnp.concatenate([stacked, next_rim], axis=-1)
        windows = cut_windows(panel, frame_rows, frame_cols, frame_side)
        patches = frame_patches(windows, probe_field, frames_in, tables)
        term = place_patches(panel.shape, patches, frame_rows, frame_cols, live_weight)
        moved = passed_along(term[..., tile_width:], "tile", 1)
        share = reduce_gradient(add_rim(term[..., :tile_width], moved))
        current = current - STEP_SIZE * share
    return current


def solution(mesh):
    in_specs = (P(("tile", "cuts"), None, None), P(), P(), P("cuts", None, None, "tile"))
    out_specs = P("cuts", None, None, "tile")
    return jax.shard_map(body, mesh=mesh, in_specs=in_specs, out_specs=out_specs, check_vma=False)
```

profile of v0, /device:TPU:0, one launch (start us, length us, event | category | flops | bytes accessed | tf_op | source)
XLA Modules:
  0.0 458.6 jit_solution(10593045391714817191)
XLA Ops:
  7.5 13.4 %all_gather.6 = bf16[4,2,256,128]{3,2,1,0:T(8,128)(2,1)S(1)} all-gather(bf16[1,2,256,128]{3,2,1,0:T(8,128)(2,1)S(1)} %convert_element_type.304), channel_id=1, replica_groups=mesh['tile'=32,'cuts'=4] {'cuts'}, dimensions={0}, use_global_device_ids=true | all-gather | bytes 655360 | tf_op jit(solution)/shard_map/all_gather | solution.py:201
  34.1 9.0 %all-to-all-start = ((f32[32,2,128,128]{3,2,1,0:T(8,128)}), f32[32,2,128,128]{3,2,1,0:T(8,128)}, u32[]{:S(2)}, u32[]{:S(2)}) async-start(f32[32,2,128,128]{3,2,1,0:T(8,128)} %broadcast_select_fusion), calls=%async_computation | async-start | bytes 8388608 | tf_op jit(solution)/shard_map/all_to_all | solution.py:180
  52.8 4.8 %scatter_custom_fusion.2 = f32[16]{0:T(128)} fusion(s32[1024]{0:T(1024)S(1)} %bitcast.768, f32[1024]{0:T(1024)S(1)} %broadcast.687, f32[]{:T(128)} %constant.180.clone.1), kind=kCustom, calls=%fused_computation.444 | custom fusion | bytes 68 | tf_op jit(solution)/shard_map/scatter | solution.py:190
  62.3 44.7 %while.2 = (s32[]{:T(128)}, bf16[4,2,256,256]{3,2,1,0:T(8,128)(2,1)S(1)}, s32[16,4]{0,1:T(4,128)S(1)}, bf16[16,4,2,128,128]{4,3,2,0,1:T(8,128)(2,1)}, s32[]{:T(128)}) while((s32[]{:T(128)}, bf16[4,2,256,256]{3,2,1,0:T(8,128)(2,1)S(1)}, s32[16,4]{0,1:T(4,128)S(1)}, bf16[16,4,2,128,128]{4,3,2,0,1:T(8,128)(2,1)}, s32[]{:T(128)}) %tuple.101), condition=%wide.while_cond, body=%wide.while_body.sunk | while | flops 2 | bytes 525937 | solution.py:102
  107.1 5.1 %bitcast_convert_fusion.20 = (f32[16,2,128,128]{3,2,1,0:T(8,128)}, f32[16,2,128,128]{3,2,1,0:T(8,128)}, f32[16,2,128,128]{3,2,1,0:T(8,128)}, f32[16,2,128,128]{3,2,1,0:T(8,128)S(1)}) fusion(bf16[16,4,2,128,128]{4,3,2,0,1:T(8,128)(2,1)} %get-tuple-element.13), kind=kLoop, calls=%fused_computation.200 | loop fusion | flops 2097152 | bytes 12582912 | tf_op jit(solution)/shard_map/convert_element_type | solution.py:92
  137.7 5.4 %add_convert_fusion.9 = (bf16[16,1,128,128]{3,2,1,0:T(8,128)(2,1)}, bf16[16,1,128,128]{3,2,1,0:T(8,128)(2,1)}, f32[16,1,128,128]{3,2,1,0:T(8,128)}, f32[16,1,128,128]{3,2,1,0:T(8,128)}) fusion(f32[16,2,128,128]{3,2,1,0:T(8,128)} %convolution_bitcast_fusion.14, f32[16,2,128,128]{3,2,1,0:T(8,128)} %get-tuple-element.99, ...), kind=kLoop, calls=%fused_computation.251 | loop fusion | flops 3670016 | bytes 9437184 | tf_op jit(solution)/shard_map/convert.26
  146.4 5.4 %add_convert_fusion.8 = (bf16[16,1,128,128]{3,2,1,0:T(8,128)(2,1)}, bf16[16,1,128,128]{3,2,1,0:T(8,128)(2,1)}, f32[16,1,128,128]{3,2,1,0:T(8,128)}, f32[16,1,128,128]{3,2,1,0:T(8,128)}) fusion(f32[16,2,128,128]{3,2,1,0:T(8,128)} %convolution_bitcast_fusion.8, f32[16,2,128,128]{3,2,1,0:T(8,128)} %get-tuple-element.100, ...), kind=kLoop, calls=%fused_computation.249 | loop fusion | flops 3670016 | bytes 9437184 | tf_op jit(solution)/shard_map/convert.24
  155.2 4.7 %add_convert_fusion.7 = (bf16[16,1,128,128]{3,2,1,0:T(8,128)(2,1)}, bf16[16,1,128,128]{3,2,1,0:T(8,128)(2,1)}, f32[16,1,128,128]{3,2,1,0:T(8,128)}, f32[16,1,128,128]{3,2,1,0:T(8,128)}) fusion(f32[16,2,128,128]{3,2,1,0:T(8,128)} %convolution_bitcast_fusion.7, f32[16,2,128,128]{3,2,1,0:T(8,128)} %get-tuple-element.101, ...), kind=kLoop, calls=%fused_computation.247 | loop fusion | flops 3670016 | bytes 9437184 | tf_op jit(solution)/shard_map/convert.22
  167.4 6.4 %fusion.359 = (bf16[16,4,2,128,128]{4,3,2,0,1:T(8,128)(2,1)}, bf16[16,4,2,128,128]{4,3,2,0,1:T(8,128)(2,1)}, bf16[16,4,2,128,128]{4,3,2,0,1:T(8,128)(2,1)}) fusion(f32[16]{0:T(128)S(1)} %copy-done.22, f32[16,1,2,128,128]{4,3,2,0,1:T(8,128)S(1)} %maximum_bitcast_fusion.3, f32[16,1,2,128,128]{4,3,2,0,1:T(8,128)S(1)} %maximum_bitcast_fusion.2, ...), kind=kLoop, calls=%fused_computation.482 | loop fusion | flops 23068672 | bytes 20971584 | tf_op jit(solution)/shard_map/convert_element_type | solution.py:125
  173.8 8.1 %fusion.8 = f32[4,2,256,256,1]{3,2,4,1,0:T(8,128)} fusion(bf16[16,4,2,128,128]{4,3,2,0,1:T(8,128)(2,1)} %get-tuple-element.61, s32[16,128]{1,0:T(8,128)S(1)} %get-tuple-element.150, s32[16,128]{1,0:T(8,128)S(1)} %copy-done.19), kind=kOutput, calls=%fused_computation.25 | convolution fusion | flops 3226468352 | bytes 6307840 | tf_op jit(solution)/shard_map/hfi,fscik->schk/dot_general | solution.py:130
  181.9 8.2 %fusion.6 = f32[4,2,256,256,1]{3,2,4,1,0:T(8,128)} fusion(bf16[16,4,2,128,128]{4,3,2,0,1:T(8,128)(2,1)} %get-tuple-element.62, s32[16,128]{1,0:T(8,128)S(1)} %get-tuple-element.150, s32[16,128]{1,0:T(8,128)S(1)} %copy-done.19), kind=kOutput, calls=%fused_computation.22 | convolution fusion | flops 3226468352 | bytes 6307840 | tf_op jit(solution)/shard_map/hfi,fscik->schk/dot_general | solution.py:130
  190.1 8.3 %fusion.39 = f32[4,2,256,256]{2,3,1,0:T(8,128)S(1)} fusion(f32[4,2,256,256,1]{3,2,4,1,0:T(8,128)} %fusion.6, f32[4,2,256,256,1]{3,2,4,1,0:T(8,128)} %fusion.8, bf16[16,4,2,128,128]{4,3,2,0,1:T(8,128)(2,1)} %get-tuple-element.60, s32[16,128]{1,0:T(8,128)S(1)} %get-tuple-element.150, s32[16,128]{1,0:T(8,128)} %get-tuple-element.151), kind=kOutput, calls=%fused_computation.70 | convolution fusion | flops 3227516928 | bytes 10502144 | tf_op jit(solution)/shard_map/hfi,fscik->schk/dot_general | solution.py:130
  205.3 36.0 %reduce-scatter.3.cloned.1.call-done = f32[1,2,256,128]{2,3,1,0:T(8,128)} async-done(((f32[4,2,256,128]{2,3,1,0:T(8,128)}), f32[1,2,256,128]{2,3,1,0:T(8,128)}) %reduce-scatter.3.cloned.1.call-update) | async-done | bytes 262160 | tf_op jit(solution)/shard_map/reduce_scatter | solution.py:137
  242.4 12.8 %all_gather.7 = bf16[4,2,256,128]{3,2,1,0:T(8,128)(2,1)S(1)} all-gather(bf16[1,2,256,128]{3,2,1,0:T(8,128)(2,1)S(1)} %copy.237), channel_id=1, replica_groups=mesh['tile'=32,'cuts'=4] {'cuts'}, dimensions={0}, use_global_device_ids=true | all-gather | bytes 655360 | tf_op jit(solution)/shard_map/all_gather | solution.py:201
  262.1 46.3 %while.3 = (s32[]{:T(128)}, bf16[4,2,256,256]{3,2,1,0:T(8,128)(2,1)S(1)}, s32[16,4]{0,1:T(4,128)S(1)}, bf16[16,4,2,128,128]{4,3,2,0,1:T(8,128)(2,1)}, s32[]{:T(128)}) while((s32[]{:T(128)}, bf16[4,2,256,256]{3,2,1,0:T(8,128)(2,1)S(1)}, s32[16,4]{0,1:T(4,128)S(1)}, bf16[16,4,2,128,128]{4,3,2,0,1:T(8,128)(2,1)}, s32[]{:T(128)}) %tuple.111), condition=%wide.while_cond.1, body=%wide.while_body.1.sunk | while | flops 2 | bytes 525937 | solution.py:102
  308.4 5.2 %bitcast_convert_fusion.16 = (f32[16,2,128,128]{3,2,1,0:T(8,128)}, f32[16,2,128,128]{3,2,1,0:T(8,128)}, f32[16,2,128,128]{3,2,1,0:T(8,128)}, f32[16,2,128,128]{3,2,1,0:T(8,128)S(1)}) fusion(bf16[16,4,2,128,128]{4,3,2,0,1:T(8,128)(2,1)} %get-tuple-element.21), kind=kLoop, calls=%fused_computation.194 | loop fusion | flops 2097152 | bytes 12582912 | tf_op jit(solution)/shard_map/convert_element_type | solution.py:92
  343.8 5.0 %add_convert_fusion.2 = (bf16[16,1,128,128]{3,2,1,0:T(8,128)(2,1)}, bf16[16,1,128,128]{3,2,1,0:T(8,128)(2,1)}, f32[16,1,128,128]{3,2,1,0:T(8,128)S(1)}, f32[16,1,128,128]{3,2,1,0:T(8,128)}) fusion(f32[16,2,128,128]{3,2,1,0:T(8,128)} %convolution_bitcast_fusion.12, f32[16,2,128,128]{3,2,1,0:T(8,128)} %get-tuple-element.77, ...), kind=kLoop, calls=%fused_computation.217 | loop fusion | flops 3670016 | bytes 9437184 | tf_op jit(solution)/shard_map/convert.12
  352.1 5.4 %add_convert_fusion.1 = (bf16[16,1,128,128]{3,2,1,0:T(8,128)(2,1)}, bf16[16,1,128,128]{3,2,1,0:T(8,128)(2,1)}, f32[16,1,128,128]{3,2,1,0:T(8,128)}, f32[16,1,128,128]{3,2,1,0:T(8,128)}) fusion(f32[16,2,128,128]{3,2,1,0:T(8,128)} %convolution_bitcast_fusion.2, f32[16,2,128,128]{3,2,1,0:T(8,128)} %get-tuple-element.78, ...), kind=kLoop, calls=%fused_computation.215 | loop fusion | flops 3670016 | bytes 9437184 | tf_op jit(solution)/shard_map/convert.10
  372.2 6.4 %fusion.358 = (bf16[16,4,2,128,128]{4,3,2,0,1:T(8,128)(2,1)}, bf16[16,4,2,128,128]{4,3,2,0,1:T(8,128)(2,1)}, bf16[16,4,2,128,128]{4,3,2,0,1:T(8,128)(2,1)}) fusion(f32[16]{0:T(128)S(1)} %copy-done.22, f32[16,1,2,128,128]{4,3,2,0,1:T(8,128)S(1)} %maximum_bitcast_fusion.7, f32[16,1,2,128,128]{4,3,2,0,1:T(8,128)S(1)} %maximum_bitcast_fusion.6, ...), kind=kLoop, calls=%fused_computation.481 | loop fusion | flops 23068672 | bytes 20971584 | tf_op jit(solution)/shard_map/convert_element_type | solution.py:125
  378.6 8.1 %fusion.2 = f32[4,2,256,256,1]{3,2,4,1,0:T(8,128)} fusion(bf16[16,4,2,128,128]{4,3,2,0,1:T(8,128)(2,1)} %get-tuple-element.58, s32[16,128]{1,0:T(8,128)S(1)} %get-tuple-element.150, s32[16,128]{1,0:T(8,128)S(1)} %copy-done.20), kind=kOutput, calls=%fused_computation.17 | convolution fusion | flops 3226468352 | bytes 6307840 | tf_op jit(solution)/shard_map/hfi,fscik->schk/dot_general | solution.py:130
  386.8 8.2 %fusion = f32[4,2,256,256,1]{3,2,4,1,0:T(8,128)} fusion(bf16[16,4,2,128,128]{4,3,2,0,1:T(8,128)(2,1)} %get-tuple-element.59, s32[16,128]{1,0:T(8,128)S(1)} %get-tuple-element.150, s32[16,128]{1,0:T(8,128)S(1)} %copy-done.20), kind=kOutput, calls=%fused_computation.14 | convolution fusion | flops 3226468352 | bytes 6307840 | tf_op jit(solution)/shard_map/hfi,fscik->schk/dot_general | solution.py:130
  395.0 8.4 %fusion.38 = f32[4,2,256,256]{2,3,1,0:T(8,128)S(1)} fusion(f32[4,2,256,256,1]{3,2,4,1,0:T(8,128)} %fusion, f32[4,2,256,256,1]{3,2,4,1,0:T(8,128)} %fusion.2, bf16[16,4,2,128,128]{4,3,2,0,1:T(8,128)(2,1)} %get-tuple-element.57, s32[16,128]{1,0:T(8,128)S(1)} %get-tuple-element.150, s32[16,128]{1,0:T(8,128)S(1)} %copy-done.20), kind=kOutput, calls=%fused_computation.65 | convolution fusion | flops 3227516928 | bytes 10502144 | tf_op jit(solution)/shard_map/hfi,fscik->schk/dot_general | solution.py:130
  403.5 8.7 %collective-permute-start.3 = (f32[4,2,256,128]{2,3,1,0:T(8,128)S(1)}, f32[4,2,256,128]{2,3,1,0:T(8,128)S(1)}, u32[]{:S(2)}, u32[]{:S(2)}) collective-permute-start(f32[4,2,256,128]{2,3,1,0:T(8,128)S(1)} %slice.507), channel_id=1, source_target_pairs={{0,4},{4,8},{8,12},{12,16},{16,20},{20,24},{24,28},{28,32},{32,36}... | collective-permute-start | bytes 3145736 | tf_op jit(solution)/shard_map/ppermute | solution.py:15
  415.6 33.9 %reduce-scatter.5.cloned.1.call-done = f32[1,2,256,128]{2,3,1,0:T(8,128)} async-done(((f32[4,2,256,128]{2,3,1,0:T(8,128)}), f32[1,2,256,128]{2,3,1,0:T(8,128)}) %reduce-scatter.5.cloned.1.call-update) | async-done | bytes 262160 | tf_op jit(solution)/shard_map/reduce_scatter | solution.py:137
  (259 shorter events, 226.9 us)
Async XLA Ops:
  20.9 38.2 %collective-permute-start = (bf16[4,2,256,128]{3,2,1,0:T(8,128)(2,1)S(1)}, bf16[4,2,256,128]{3,2,1,0:T(8,128)(2,1)S(1)}, u32[]{:S(2)}, u32[]{:S(2)}) collective-permute-start(bf16[4,2,256,128]{3,2,1,0:T(8,128)(2,1)S(1)} %all_gather.6), channel_id=1, source_target_pairs={{4,0},{8,4},{12,8},{16,12},{20,16},{24,20},{28,24},{32,28},{36,32}... | collective-permute-start | bytes 1572872 | tf_op jit(solution)/shard_map/ppermute | solution.py:15
  34.1 93.5 %all-to-all-start = ((f32[32,2,128,128]{3,2,1,0:T(8,128)}), f32[32,2,128,128]{3,2,1,0:T(8,128)}, u32[]{:S(2)}, u32[]{:S(2)}) async-start(f32[32,2,128,128]{3,2,1,0:T(8,128)} %broadcast_select_fusion), calls=%async_computation | async-start | bytes 8388608 | tf_op jit(solution)/shard_map/all_to_all | solution.py:180
  43.1 198.1 %reduce-scatter.3.cloned.1.call-start = ((), (), s32[]{:S(2)}) async-start(), calls=%async_computation.3 | async-start | bytes 1310720 | tf_op jit(solution)/shard_map/reduce_scatter | solution.py:137
  43.8 15.3 %copy-start.18 = (f32[2,128,128]{2,1,0:T(8,128)S(1)}, f32[2,128,128]{2,1,0:T(8,128)}, u32[]{:S(2)}) copy-start(f32[2,128,128]{2,1,0:T(8,128)} %param.8) | copy-start | bytes 393220
  162.1 1.2 copy-start.9
  162.1 1.5 copy-start.10
  163.6 1.5 copy-start.6
  165.2 1.5 copy-start.2
  167.4 6.4 %copy-start.19 = (s32[16,128]{1,0:T(8,128)S(1)}, s32[16,128]{1,0:T(8,128)}, u32[]{:S(2)}) copy-start(s32[16,128]{1,0:T(8,128)} %get-tuple-element.151) | copy-start | bytes 24580
  198.6 4.4 collective-permute-start.1
  204.1 245.3 %reduce-scatter.5.cloned.1.call-start = ((), (), s32[]{:S(2)}) async-start(), calls=%async_computation.4 | async-start | bytes 1310720 | tf_op jit(solution)/shard_map/reduce_scatter | solution.py:137
  205.3 51.2 %copy-start.11 = (f32[1,2,256,128]{2,3,1,0:T(8,128)}, f32[1,2,256,128]{2,3,1,0:T(8,128)S(1)}, u32[]{:S(2)}) copy-start(f32[1,2,256,128]{2,3,1,0:T(8,128)S(1)} %copy.236) | copy-start | bytes 786436
  255.2 3.8 collective-permute-start.2
  329.9 3.6 copy-start.15
  329.9 3.6 copy-start.16
  333.4 3.3 copy-start.21
  336.8 3.1 copy-start.13
  336.8 3.1 copy-start.14
  367.7 1.5 copy-start.8
  369.2 1.5 copy-start.4
  372.2 6.4 %copy-start.20 = (s32[16,128]{1,0:T(8,128)S(1)}, s32[16,128]{1,0:T(8,128)}, u32[]{:S(2)}) copy-start(s32[16,128]{1,0:T(8,128)} %get-tuple-element.151) | copy-start | bytes 24580
  403.5 46.0 %copy-start.12 = (f32[1,2,256,128]{2,3,1,0:T(8,128)S(1)}, f32[1,2,256,128]{2,3,1,0:T(8,128)}, u32[]{:S(2)}) copy-start(f32[1,2,256,128]{2,3,1,0:T(8,128)} %copy-done.11) | copy-start | bytes 786436
  403.5 46.0 %copy-start.17 = (f32[1,2,256,128]{2,3,1,0:T(8,128)S(1)}, f32[1,2,256,128]{2,3,1,0:T(8,128)}, u32[]{:S(2)}) copy-start(f32[1,2,256,128]{2,3,1,0:T(8,128)} %reduce-scatter.3.cloned.1.call-done) | copy-start | bytes 786436
  403.5 10.9 %collective-permute-start.3 = (f32[4,2,256,128]{2,3,1,0:T(8,128)S(1)}, f32[4,2,256,128]{2,3,1,0:T(8,128)S(1)}, u32[]{:S(2)}, u32[]{:S(2)}) collective-permute-start(f32[4,2,256,128]{2,3,1,0:T(8,128)S(1)} %slice.507), channel_id=1, source_target_pairs={{0,4},{4,8},{8,12},{12,16},{16,20},{20,24},{24,28},{28,32},{32,36}... | collective-permute-start | bytes 3145736 | tf_op jit(solution)/shard_map/ppermute | solution.py:15
  (6 other events, 6.8 us)
Sparse Core Ops, SparseCore 0:
  204.3 36.9 reduce-scatter.2
  415.7 33.6 reduce-scatter.4
where the time goes:
time: 466 us; the launch traced here: 459 us
  local copies, waits for them, and re-layouts  127 us (27%)
  matrix products  96.5 us (21%)
  other arithmetic  95.2 us (20%)
  waiting for transfers between devices  76.8 us (16%)
  blocking collectives  26.2 us (6%)
  starting transfers between devices  22.6 us (5%)
  between operations  14.4 us (3%)
    gather x96, local copies, waits for them, and re-layouts  90.8 us
    reduce_scatter x2, waiting for transfers between devices, reduce_gradient(): return lax.psum_scatter(term_part, 'cuts', scatter_dimension=0, tiled=True)  69.8 us
    another operation x18, other arithmetic  50.1 us
    dot_general x6, matrix products, place_patches(): jnp.einsum('hfi,fscik->schk', row_onehot, placed_cols, preferred_element_...  49.4 us
    dot_general x16, matrix products, right_product(): jnp.einsum('fcij,cjdk->fdik', field.astype(jnp.bfloat16), table, preferre...  45.2 us
    all_gather x2, blocking collectives, body(): lax.all_gather(current.astype(jnp.bfloat16), 'cuts', axis=0, tiled=True)  26.2 us
    unnamed x49, local copies, waits for them, and re-layouts  15.1 us
    ppermute x4, starting transfers between devices, passed_along(): return lax.ppermute(x, axis, pairs)  13.5 us
  transfers between devices with their start and end apart: 7, of which 5 were waited for; matrix products, arithmetic and copies ran while one was open for 21% of the time, Pallas kernels for 0%

commit v1 on v0

--- a/solution.py
+++ b/solution.py
@@ -7,6 +7,24 @@
 ITERS = 2
 STEP_SIZE = 0.05
 AMPLITUDE_FLOOR = 0.25
+
+
+def collect(value, axis, dim):
+    ways, here, step = (lax.axis_size(axis), lax.axis_index(axis), value.shape[dim])
+    shape = [n * ways if d == dim else n for d, n in enumerate(value.shape)]
+    full = lax.dynamic_update_slice_in_dim(
+        jnp.zeros(shape, value.dtype), value, here * step, axis=dim
+    )
+    going_up = going_down = value
+    for far in range(1, ways // 2 + 1):
+        going_up = lax.ppermute(going_up, axis, [(d, (d + 1) % ways) for d in range(ways)])
+        full = lax.dynamic_update_slice_in_dim(full, going_up, (here - far) % ways * step, axis=dim)
+        if 2 * far < ways:
+            going_down = lax.ppermute(going_down, axis, [(d, (d - 1) % ways) for d in range(ways)])
+            full = lax.dynamic_update_slice_in_dim(
+                full, going_down, (here + far) % ways * step, axis=dim
+            )
+    return full
 
 
 def passed_along(x, axis, by):
@@ -198,7 +216,7 @@
     tables = make_tables(frame_side)
     current = object_slices
     for turn in range(ITERS):
-        stacked = lax.all_gather(current.astype(jnp.bfloat16), "cuts", axis=0, tiled=True)
+        stacked = collect(current.astype(jnp.bfloat16), "cuts", 0)
         next_rim = passed_along(stacked, "tile", -1)
         panel = jnp.concatenate([stacked, next_rim], axis=-1)
         windows = cut_windows(panel, frame_rows, frame_cols, frame_side)

time: 466 us -> 488 us (1.047)
  starting transfers between devices: 22.6 us -> 58.7 us
  blocking collectives: 26.2 us -> 0 us
  waiting for transfers between devices: 76.8 us -> 89.2 us
    ppermute x4, starting transfers between devices: 13.5 us -> 43.1 us  [passed_along(): return lax.ppermute(x, axis, pairs)]
    all_gather x2 -> x0, blocking collectives: 26.2 us -> none  [body(): lax.all_gather(current.astype(jnp.bfloat16), 'cuts', axis=0, tiled=True)]
    ppermute x0 -> x6, waiting for transfers between devices: none -> 15 us  [the longest x4 15 us: collect(): lax.ppermute(going_up, axis, [(d, (d + 1) % ways) for d in range(ways)])]
    ppermute x0 -> x6, starting transfers between devices: none -> 7.11 us  [the longest x2 4.84 us: collect(): lax.ppermute(going_down, axis, [(d, (d - 1) % ways) for d in range(ways)])]
  transfers between devices with their start and end apart: 7 -> 13, of which waited for: 5 -> 9; matrix products, arithmetic and copies ran while one was open for 21% -> 21% of each run, Pallas kernels for 0% -> 0%
where the time goes in v1:
time: 488 us; the launch traced here: 479 us
  local copies, waits for them, and re-layouts  125 us (26%)
  matrix products  96.3 us (20%)
  other arithmetic  95.5 us (20%)
  waiting for transfers between devices  89.2 us (18%)
  starting transfers between devices  58.7 us (12%)
  between operations  14.5 us (3%)
    gather x96, local copies, waits for them, and re-layouts  88.1 us
    reduce_scatter x2, waiting for transfers between devices, reduce_gradient(): return lax.psum_scatter(term_part, 'cuts', scatter_dimension=0, tiled=True)  65.4 us
    another operation x18, other arithmetic  50.3 us
    dot_general x6, matrix products, place_patches(): jnp.einsum('hfi,fscik->schk', row_onehot, placed_cols, preferred_element_...  49.3 us
    dot_general x16, matrix products, right_product(): jnp.einsum('fcij,cjdk->fdik', field.astype(jnp.bfloat16), table, preferre...  45.2 us
    ppermute x4, starting transfers between devices, passed_along(): return lax.ppermute(x, axis, pairs)  43.1 us
    unnamed x49, local copies, waits for them, and re-layouts  15.1 us
    ppermute x4, waiting for transfers between devices, collect(): lax.ppermute(going_up, axis, [(d, (d + 1) % ways) for d in range(ways)])  15 us
  transfers between devices with their start and end apart: 13, of which 9 were waited for; matrix products, arithmetic and copies ran while one was open for 21% of the time, Pallas kernels for 0%

profile of v1, /device:TPU:0, one launch (start us, length us, event | category | flops | bytes accessed | tf_op | source)
XLA Modules:
  0.0 479.1 jit_solution(5398144170445806705)
XLA Ops:
  22.8 8.4 %all-to-all-start = ((f32[32,2,128,128]{3,2,1,0:T(8,128)}), f32[32,2,128,128]{3,2,1,0:T(8,128)}, u32[]{:S(2)}, u32[]{:S(2)}) async-start(f32[32,2,128,128]{3,2,1,0:T(8,128)} %broadcast_select_fusion), calls=%async_computation | async-start | bytes 8388608 | tf_op jit(solution)/shard_map/all_to_all | solution.py:198
  41.8 4.8 scatter_custom_fusion.2
  47.0 6.4 %collective-permute-done.2 = bf16[1,2,256,128]{3,2,1,0:T(8,128)(2,1)S(1)} collective-permute-done((bf16[1,2,256,128]{3,2,1,0:T(8,128)(2,1)S(1)}, bf16[1,2,256,128]{3,2,1,0:T(8,128)(2,1)S(1)}, u32[]{:S(2)}, u32[]{:S(2)}) %collective-permute-start.2) | collective-permute-done | bytes 131104 | tf_op jit(solution)/shard_map/ppermute | solution.py:20
  60.4 45.9 %while.2 = (s32[]{:T(128)}, bf16[4,2,256,256]{3,2,1,0:T(8,128)(2,1)S(1)}, s32[16,4]{0,1:T(4,128)S(1)}, bf16[16,4,2,128,128]{4,3,2,0,1:T(8,128)(2,1)}, s32[]{:T(128)}) while((s32[]{:T(128)}, bf16[4,2,256,256]{3,2,1,0:T(8,128)(2,1)S(1)}, s32[16,4]{0,1:T(4,128)S(1)}, bf16[16,4,2,128,128]{4,3,2,0,1:T(8,128)(2,1)}, s32[]{:T(128)}) %tuple.100), condition=%wide.while_cond, body=%wide.while_body.sunk | while | flops 2 | bytes 525937 | solution.py:120
  106.3 5.1 %bitcast_convert_fusion.20 = (f32[16,2,128,128]{3,2,1,0:T(8,128)}, f32[16,2,128,128]{3,2,1,0:T(8,128)}, f32[16,2,128,128]{3,2,1,0:T(8,128)}, f32[16,2,128,128]{3,2,1,0:T(8,128)S(1)}) fusion(bf16[16,4,2,128,128]{4,3,2,0,1:T(8,128)(2,1)} %get-tuple-element.13), kind=kLoop, calls=%fused_computation.200 | loop fusion | flops 2097152 | bytes 12582912 | tf_op jit(solution)/shard_map/convert_element_type | solution.py:110
  136.8 5.5 %add_convert_fusion.9 = (bf16[16,1,128,128]{3,2,1,0:T(8,128)(2,1)}, bf16[16,1,128,128]{3,2,1,0:T(8,128)(2,1)}, f32[16,1,128,128]{3,2,1,0:T(8,128)}, f32[16,1,128,128]{3,2,1,0:T(8,128)}) fusion(f32[16,2,128,128]{3,2,1,0:T(8,128)} %convolution_bitcast_fusion.14, f32[16,2,128,128]{3,2,1,0:T(8,128)} %get-tuple-element.93, ...), kind=kLoop, calls=%fused_computation.251 | loop fusion | flops 3670016 | bytes 9437184 | tf_op jit(solution)/shard_map/convert.26
  145.7 5.5 %add_convert_fusion.8 = (bf16[16,1,128,128]{3,2,1,0:T(8,128)(2,1)}, bf16[16,1,128,128]{3,2,1,0:T(8,128)(2,1)}, f32[16,1,128,128]{3,2,1,0:T(8,128)}, f32[16,1,128,128]{3,2,1,0:T(8,128)}) fusion(f32[16,2,128,128]{3,2,1,0:T(8,128)} %convolution_bitcast_fusion.8, f32[16,2,128,128]{3,2,1,0:T(8,128)} %get-tuple-element.94, ...), kind=kLoop, calls=%fused_computation.249 | loop fusion | flops 3670016 | bytes 9437184 | tf_op jit(solution)/shard_map/convert.24
  166.7 6.4 %fusion.359 = (bf16[16,4,2,128,128]{4,3,2,0,1:T(8,128)(2,1)}, bf16[16,4,2,128,128]{4,3,2,0,1:T(8,128)(2,1)}, bf16[16,4,2,128,128]{4,3,2,0,1:T(8,128)(2,1)}) fusion(f32[16]{0:T(128)S(1)} %copy-done.22, f32[16,1,2,128,128]{4,3,2,0,1:T(8,128)S(1)} %maximum_bitcast_fusion.3, f32[16,1,2,128,128]{4,3,2,0,1:T(8,128)S(1)} %maximum_bitcast_fusion.2, ...), kind=kLoop, calls=%fused_computation.490 | loop fusion | flops 23068672 | bytes 20971584 | tf_op jit(solution)/shard_map/convert_element_type | solution.py:143
  173.1 8.1 %fusion.8 = f32[4,2,256,256,1]{3,2,4,1,0:T(8,128)} fusion(bf16[16,4,2,128,128]{4,3,2,0,1:T(8,128)(2,1)} %get-tuple-element.55, s32[16,128]{1,0:T(8,128)S(1)} %get-tuple-element.144, s32[16,128]{1,0:T(8,128)S(1)} %copy-done.19), kind=kOutput, calls=%fused_computation.25 | convolution fusion | flops 3226468352 | bytes 6307840 | tf_op jit(solution)/shard_map/hfi,fscik->schk/dot_general | solution.py:148
  181.2 8.2 %fusion.6 = f32[4,2,256,256,1]{3,2,4,1,0:T(8,128)} fusion(bf16[16,4,2,128,128]{4,3,2,0,1:T(8,128)(2,1)} %get-tuple-element.56, s32[16,128]{1,0:T(8,128)S(1)} %get-tuple-element.144, s32[16,128]{1,0:T(8,128)S(1)} %copy-done.19), kind=kOutput, calls=%fused_computation.22 | convolution fusion | flops 3226468352 | bytes 6307840 | tf_op jit(solution)/shard_map/hfi,fscik->schk/dot_general | solution.py:148
  189.4 8.3 %fusion.39 = f32[4,2,256,256]{2,3,1,0:T(8,128)S(1)} fusion(f32[4,2,256,256,1]{3,2,4,1,0:T(8,128)} %fusion.6, f32[4,2,256,256,1]{3,2,4,1,0:T(8,128)} %fusion.8, bf16[16,4,2,128,128]{4,3,2,0,1:T(8,128)(2,1)} %get-tuple-element.54, s32[16,128]{1,0:T(8,128)S(1)} %get-tuple-element.144, s32[16,128]{1,0:T(8,128)} %get-tuple-element.145), kind=kOutput, calls=%fused_computation.70 | convolution fusion | flops 3227516928 | bytes 10502144 | tf_op jit(solution)/shard_map/hfi,fscik->schk/dot_general | solution.py:148
  197.8 31.7 %collective-permute-start.4 = (f32[4,2,256,128]{2,3,1,0:T(8,128)S(1)}, f32[4,2,256,128]{2,3,1,0:T(8,128)S(1)}, u32[]{:S(2)}, u32[]{:S(2)}) collective-permute-start(f32[4,2,256,128]{2,3,1,0:T(8,128)S(1)} %slice.481), channel_id=1, source_target_pairs={{0,4},{4,8},{8,12},{12,16},{16,20},{20,24},{24,28},{28,32},{32,36}... | collective-permute-start | bytes 3145736 | tf_op jit(solution)/shard_map/ppermute | solution.py:33
  234.1 32.5 %reduce-scatter.3.cloned.1.call-done = f32[1,2,256,128]{2,3,1,0:T(8,128)} async-done(((f32[4,2,256,128]{2,3,1,0:T(8,128)}), f32[1,2,256,128]{2,3,1,0:T(8,128)}) %reduce-scatter.3.cloned.1.call-update) | async-done | bytes 262160 | tf_op jit(solution)/shard_map/reduce_scatter | solution.py:155
  274.2 6.0 %collective-permute-done.7 = bf16[1,2,256,128]{2,3,1,0:T(8,128)(2,1)S(1)} collective-permute-done((bf16[1,2,256,128]{2,3,1,0:T(8,128)(2,1)S(1)}, bf16[1,2,256,128]{2,3,1,0:T(8,128)(2,1)S(1)}, u32[]{:S(2)}, u32[]{:S(2)}) %collective-permute-start.7) | collective-permute-done | bytes 131104 | tf_op jit(solution)/shard_map/ppermute | solution.py:20
  287.3 42.4 %while.3 = (s32[]{:T(128)}, bf16[4,2,256,256]{3,2,1,0:T(8,128)(2,1)S(1)}, s32[16,4]{0,1:T(4,128)S(1)}, bf16[16,4,2,128,128]{4,3,2,0,1:T(8,128)(2,1)}, s32[]{:T(128)}) while((s32[]{:T(128)}, bf16[4,2,256,256]{3,2,1,0:T(8,128)(2,1)S(1)}, s32[16,4]{0,1:T(4,128)S(1)}, bf16[16,4,2,128,128]{4,3,2,0,1:T(8,128)(2,1)}, s32[]{:T(128)}) %tuple.110), condition=%wide.while_cond.1, body=%wide.while_body.1.sunk | while | flops 2 | bytes 525937 | solution.py:120
  329.7 5.2 %bitcast_convert_fusion.16 = (f32[16,2,128,128]{3,2,1,0:T(8,128)}, f32[16,2,128,128]{3,2,1,0:T(8,128)}, f32[16,2,128,128]{3,2,1,0:T(8,128)}, f32[16,2,128,128]{3,2,1,0:T(8,128)S(1)}) fusion(bf16[16,4,2,128,128]{4,3,2,0,1:T(8,128)(2,1)} %get-tuple-element.21), kind=kLoop, calls=%fused_computation.194 | loop fusion | flops 2097152 | bytes 12582912 | tf_op jit(solution)/shard_map/convert_element_type | solution.py:110
  365.2 5.0 %add_convert_fusion.2 = (bf16[16,1,128,128]{3,2,1,0:T(8,128)(2,1)}, bf16[16,1,128,128]{3,2,1,0:T(8,128)(2,1)}, f32[16,1,128,128]{3,2,1,0:T(8,128)S(1)}, f32[16,1,128,128]{3,2,1,0:T(8,128)}) fusion(f32[16,2,128,128]{3,2,1,0:T(8,128)} %convolution_bitcast_fusion.12, f32[16,2,128,128]{3,2,1,0:T(8,128)} %get-tuple-element.71, ...), kind=kLoop, calls=%fused_computation.217 | loop fusion | flops 3670016 | bytes 9437184 | tf_op jit(solution)/shard_map/convert.12
  373.5 5.4 %add_convert_fusion.1 = (bf16[16,1,128,128]{3,2,1,0:T(8,128)(2,1)}, bf16[16,1,128,128]{3,2,1,0:T(8,128)(2,1)}, f32[16,1,128,128]{3,2,1,0:T(8,128)}, f32[16,1,128,128]{3,2,1,0:T(8,128)}) fusion(f32[16,2,128,128]{3,2,1,0:T(8,128)} %convolution_bitcast_fusion.2, f32[16,2,128,128]{3,2,1,0:T(8,128)} %get-tuple-element.72, ...), kind=kLoop, calls=%fused_computation.215 | loop fusion | flops 3670016 | bytes 9437184 | tf_op jit(solution)/shard_map/convert.10
  393.6 6.4 %fusion.358 = (bf16[16,4,2,128,128]{4,3,2,0,1:T(8,128)(2,1)}, bf16[16,4,2,128,128]{4,3,2,0,1:T(8,128)(2,1)}, bf16[16,4,2,128,128]{4,3,2,0,1:T(8,128)(2,1)}) fusion(f32[16]{0:T(128)S(1)} %copy-done.22, f32[16,1,2,128,128]{4,3,2,0,1:T(8,128)S(1)} %maximum_bitcast_fusion.7, f32[16,1,2,128,128]{4,3,2,0,1:T(8,128)S(1)} %maximum_bitcast_fusion.6, ...), kind=kLoop, calls=%fused_computation.489 | loop fusion | flops 23068672 | bytes 20971584 | tf_op jit(solution)/shard_map/convert_element_type | solution.py:143
  400.1 8.1 %fusion.2 = f32[4,2,256,256,1]{3,2,4,1,0:T(8,128)} fusion(bf16[16,4,2,128,128]{4,3,2,0,1:T(8,128)(2,1)} %get-tuple-element.52, s32[16,128]{1,0:T(8,128)S(1)} %get-tuple-element.144, s32[16,128]{1,0:T(8,128)S(1)} %copy-done.20), kind=kOutput, calls=%fused_computation.17 | convolution fusion | flops 3226468352 | bytes 6307840 | tf_op jit(solution)/shard_map/hfi,fscik->schk/dot_general | solution.py:148
  408.2 8.2 %fusion = f32[4,2,256,256,1]{3,2,4,1,0:T(8,128)} fusion(bf16[16,4,2,128,128]{4,3,2,0,1:T(8,128)(2,1)} %get-tuple-element.53, s32[16,128]{1,0:T(8,128)S(1)} %get-tuple-element.144, s32[16,128]{1,0:T(8,128)S(1)} %copy-done.20), kind=kOutput, calls=%fused_computation.14 | convolution fusion | flops 3226468352 | bytes 6307840 | tf_op jit(solution)/shard_map/hfi,fscik->schk/dot_general | solution.py:148
  416.3 8.4 %fusion.38 = f32[4,2,256,256]{2,3,1,0:T(8,128)S(1)} fusion(f32[4,2,256,256,1]{3,2,4,1,0:T(8,128)} %fusion, f32[4,2,256,256,1]{3,2,4,1,0:T(8,128)} %fusion.2, bf16[16,4,2,128,128]{4,3,2,0,1:T(8,128)(2,1)} %get-tuple-element.51, s32[16,128]{1,0:T(8,128)S(1)} %get-tuple-element.144, s32[16,128]{1,0:T(8,128)S(1)} %copy-done.20), kind=kOutput, calls=%fused_computation.65 | convolution fusion | flops 3227516928 | bytes 10502144 | tf_op jit(solution)/shard_map/hfi,fscik->schk/dot_general | solution.py:148
  424.8 8.8 %collective-permute-start.9 = (f32[4,2,256,128]{2,3,1,0:T(8,128)S(1)}, f32[4,2,256,128]{2,3,1,0:T(8,128)S(1)}, u32[]{:S(2)}, u32[]{:S(2)}) collective-permute-start(f32[4,2,256,128]{2,3,1,0:T(8,128)S(1)} %slice.507), channel_id=1, source_target_pairs={{0,4},{4,8},{8,12},{12,16},{16,20},{20,24},{24,28},{28,32},{32,36}... | collective-permute-start | bytes 3145736 | tf_op jit(solution)/shard_map/ppermute | solution.py:33
  437.1 32.9 %reduce-scatter.5.cloned.1.call-done = f32[1,2,256,128]{2,3,1,0:T(8,128)} async-done(((f32[4,2,256,128]{2,3,1,0:T(8,128)}), f32[1,2,256,128]{2,3,1,0:T(8,128)}) %reduce-scatter.5.cloned.1.call-update) | async-done | bytes 262160 | tf_op jit(solution)/shard_map/reduce_scatter | solution.py:155
  (281 shorter events, 239.2 us)
Async XLA Ops:
  7.6 38.9 %collective-permute-start = (bf16[1,2,256,128]{3,2,1,0:T(8,128)(2,1)S(1)}, bf16[1,2,256,128]{3,2,1,0:T(8,128)(2,1)S(1)}, u32[]{:S(2)}, u32[]{:S(2)}) collective-permute-start(bf16[1,2,256,128]{3,2,1,0:T(8,128)(2,1)S(1)} %get-tuple-element.46), channel_id=1, source_target_pairs={{0,1},{1,2},{2,3},{3,0},{4,5},{5,6},{6,7},{7,4},{8,9},{9,10},{10,1... | collective-permute-start | bytes 393224 | tf_op jit(solution)/shard_map/ppermute | solution.py:20
  9.4 37.6 %collective-permute-start.1 = (bf16[1,2,256,128]{3,2,1,0:T(8,128)(2,1)S(1)}, bf16[1,2,256,128]{3,2,1,0:T(8,128)(2,1)S(1)}, u32[]{:S(2)}, u32[]{:S(2)}) collective-permute-start(bf16[1,2,256,128]{3,2,1,0:T(8,128)(2,1)S(1)} %get-tuple-element.46), channel_id=1, source_target_pairs={{0,3},{1,0},{2,1},{3,2},{4,7},{5,4},{6,5},{7,6},{8,11},{9,8},{10,9... | collective-permute-start | bytes 393224 | tf_op jit(solution)/shard_map/ppermute | solution.py:23
  22.8 104.1 %all-to-all-start = ((f32[32,2,128,128]{3,2,1,0:T(8,128)}), f32[32,2,128,128]{3,2,1,0:T(8,128)}, u32[]{:S(2)}, u32[]{:S(2)}) async-start(f32[32,2,128,128]{3,2,1,0:T(8,128)} %broadcast_select_fusion), calls=%async_computation | async-start | bytes 8388608 | tf_op jit(solution)/shard_map/all_to_all | solution.py:198
  31.2 235.4 %reduce-scatter.3.cloned.1.call-start = ((), (), s32[]{:S(2)}) async-start(), calls=%async_computation.3 | async-start | bytes 1310720 | tf_op jit(solution)/shard_map/reduce_scatter | solution.py:155
  37.7 17.6 %copy-start.18 = (f32[2,128,128]{2,1,0:T(8,128)S(1)}, f32[2,128,128]{2,1,0:T(8,128)}, u32[]{:S(2)}) copy-start(f32[2,128,128]{2,1,0:T(8,128)} %param.8) | copy-start | bytes 393220
  46.6 6.8 %collective-permute-start.2 = (bf16[1,2,256,128]{3,2,1,0:T(8,128)(2,1)S(1)}, bf16[1,2,256,128]{3,2,1,0:T(8,128)(2,1)S(1)}, u32[]{:S(2)}, u32[]{:S(2)}) collective-permute-start(bf16[1,2,256,128]{3,2,1,0:T(8,128)(2,1)S(1)} %collective-permute-done), channel_id=1, source_target_pairs={{0,1},{1,2},{2,3},{3,0},{4,5},{5,6},{6,7},{7,4},{8,9},{9,10},{10,1... | collective-permute-start | bytes 393224 | tf_op jit(solution)/shard_map/ppermute | solution.py:20
  53.4 3.8 collective-permute-start.3
  166.7 6.4 %copy-start.19 = (s32[16,128]{1,0:T(8,128)S(1)}, s32[16,128]{1,0:T(8,128)}, u32[]{:S(2)}) copy-start(s32[16,128]{1,0:T(8,128)} %get-tuple-element.145) | copy-start | bytes 24580
  197.8 33.9 %collective-permute-start.4 = (f32[4,2,256,128]{2,3,1,0:T(8,128)S(1)}, f32[4,2,256,128]{2,3,1,0:T(8,128)S(1)}, u32[]{:S(2)}, u32[]{:S(2)}) collective-permute-start(f32[4,2,256,128]{2,3,1,0:T(8,128)S(1)} %slice.481), channel_id=1, source_target_pairs={{0,4},{4,8},{8,12},{12,16},{16,20},{20,24},{24,28},{28,32},{32,36}... | collective-permute-start | bytes 3145736 | tf_op jit(solution)/shard_map/ppermute | solution.py:33
  233.0 237.1 %reduce-scatter.5.cloned.1.call-start = ((), (), s32[]{:S(2)}) async-start(), calls=%async_computation.4 | async-start | bytes 1310720 | tf_op jit(solution)/shard_map/reduce_scatter | solution.py:155
  234.1 47.6 %copy-start.11 = (f32[1,2,256,128]{2,3,1,0:T(8,128)}, f32[1,2,256,128]{2,3,1,0:T(8,128)S(1)}, u32[]{:S(2)}) copy-start(f32[1,2,256,128]{2,3,1,0:T(8,128)S(1)} %copy.177) | copy-start | bytes 786436
  267.6 6.2 %collective-permute-start.5 = (bf16[1,2,256,128]{2,3,1,0:T(8,128)(2,1)S(1)}, bf16[1,2,256,128]{2,3,1,0:T(8,128)(2,1)S(1)}, u32[]{:S(2)}, u32[]{:S(2)}) collective-permute-start(bf16[1,2,256,128]{2,3,1,0:T(8,128)(2,1)S(1)} %fusion.222), channel_id=1, source_target_pairs={{0,1},{1,2},{2,3},{3,0},{4,5},{5,6},{6,7},{7,4},{8,9},{9,10},{10,1... | collective-permute-start | bytes 393224 | tf_op jit(solution)/shard_map/ppermute | solution.py:20
  267.8 6.3 %collective-permute-start.6 = (bf16[1,2,256,128]{2,3,1,0:T(8,128)(2,1)S(1)}, bf16[1,2,256,128]{2,3,1,0:T(8,128)(2,1)S(1)}, u32[]{:S(2)}, u32[]{:S(2)}) collective-permute-start(bf16[1,2,256,128]{2,3,1,0:T(8,128)(2,1)S(1)} %fusion.222), channel_id=1, source_target_pairs={{0,3},{1,0},{2,1},{3,2},{4,7},{5,4},{6,5},{7,6},{8,11},{9,8},{10,9... | collective-permute-start | bytes 393224 | tf_op jit(solution)/shard_map/ppermute | solution.py:23
  273.9 6.2 %collective-permute-start.7 = (bf16[1,2,256,128]{2,3,1,0:T(8,128)(2,1)S(1)}, bf16[1,2,256,128]{2,3,1,0:T(8,128)(2,1)S(1)}, u32[]{:S(2)}, u32[]{:S(2)}) collective-permute-start(bf16[1,2,256,128]{2,3,1,0:T(8,128)(2,1)S(1)} %collective-permute-done.5), channel_id=1, source_target_pairs={{0,1},{1,2},{2,3},{3,0},{4,5},{5,6},{6,7},{7,4},{8,9},{9,10},{10,1... | collective-permute-start | bytes 393224 | tf_op jit(solution)/shard_map/ppermute | solution.py:20
  280.3 3.8 collective-permute-start.8
  351.2 3.6 copy-start.15
  351.2 3.6 copy-start.16
  354.8 3.4 copy-start.21
  358.2 3.1 copy-start.13
  358.2 3.1 copy-start.14
  393.6 6.4 %copy-start.20 = (s32[16,128]{1,0:T(8,128)S(1)}, s32[16,128]{1,0:T(8,128)}, u32[]{:S(2)}) copy-start(s32[16,128]{1,0:T(8,128)} %get-tuple-element.145) | copy-start | bytes 24580
  424.8 45.2 %copy-start.12 = (f32[1,2,256,128]{2,3,1,0:T(8,128)S(1)}, f32[1,2,256,128]{2,3,1,0:T(8,128)}, u32[]{:S(2)}) copy-start(f32[1,2,256,128]{2,3,1,0:T(8,128)} %copy-done.11) | copy-start | bytes 786436
  424.8 45.2 %copy-start.17 = (f32[1,2,256,128]{2,3,1,0:T(8,128)S(1)}, f32[1,2,256,128]{2,3,1,0:T(8,128)}, u32[]{:S(2)}) copy-start(f32[1,2,256,128]{2,3,1,0:T(8,128)} %reduce-scatter.3.cloned.1.call-done) | copy-start | bytes 786436
  424.8 11.0 %collective-permute-start.9 = (f32[4,2,256,128]{2,3,1,0:T(8,128)S(1)}, f32[4,2,256,128]{2,3,1,0:T(8,128)S(1)}, u32[]{:S(2)}, u32[]{:S(2)}) collective-permute-start(f32[4,2,256,128]{2,3,1,0:T(8,128)S(1)} %slice.507), channel_id=1, source_target_pairs={{0,4},{4,8},{8,12},{12,16},{16,20},{20,24},{24,28},{28,32},{32,36}... | collective-permute-start | bytes 3145736 | tf_op jit(solution)/shard_map/ppermute | solution.py:33
  (12 other events, 15.7 us)
Sparse Core Ops, SparseCore 0:
  233.1 33.4 reduce-scatter.2
  437.2 32.7 reduce-scatter.4
